TPU v7x, 32 devices: a whole 2x2x4 slice. The times are simulated.
32 devices in a mesh: row: 4 (over y, x), col: 8 (over z, core).
Axes of the slice: x: 2, y: 2, z: 4, core: 2. Of those that a mesh axis runs over, the one named last changes fastest.
Arguments:
- legendre: bfloat16 [512, 512, 512], P('row', 'col'), may hold values from -6 to 6
- vectors: bfloat16 [512, 512, 256], P('row', 'col'), may hold values from -6 to 6
- panel_orders: int32 [4], replicated, may hold values from 0 to 511, as said below
- cycle_span: int32 [512, 2], replicated, may hold values from 0 to 2047, as said below
- cycle_weight: float32 [512], replicated, may hold values from 0.0009765625 to 0.0029296875
Outputs:
- projected: bfloat16 [512, 4, 256], P('col', 'row')
Inputs may be any that keep to these rules, and one draw needn't show every extreme that they name: `panel_orders`: the 4 entries are distinct orders; 0 and 511 are among them. `cycle_span`: in every cycle the first entry is smaller than the second.
All inputs are finite; a program needn't handle non-finite values.
Results may differ from a plain program's by a relative error of at most 0.008.
Values may be sent and summed in bfloat16 or wider, within the bound.
A program may use at most 64 MiB of HBM per device.

v0:
```python
import functools
import math

import jax
import jax.numpy as jnp
from jax import lax
from jax.experimental import pallas as pl
from jax.experimental.pallas import tpu as pltpu
from jax.sharding import PartitionSpec as P

NPHI = 2048
MESH = pl.DeviceIdType.MESH
BF16 = jnp.bfloat16
F32 = jnp.float32


def sine_pair(orders, cells):
    angle = (2.0 * math.pi / NPHI) * (orders[:, None] * cells[None, :] % NPHI).astype(F32)
    return jnp.sin(angle), jnp.cos(angle)


def order_sines(first_order, ord_count, cells):
    step = 16
    high_sin, high_cos = sine_pair(first_order + step * jnp.arange(ord_count // step, dtype=jnp.int32), cells)
    low_sin, low_cos = sine_pair(jnp.arange(step, dtype=jnp.int32), cells)
    high_sin, high_cos = high_sin[:, None], high_cos[:, None]
    low_sin, low_cos = low_sin[None], low_cos[None]
    shape = (ord_count, cells.shape[0])
    sines = (high_sin * low_cos + high_cos * low_sin).reshape(shape)
    cosines = (high_cos * low_cos - high_sin * low_sin).reshape(shape)
    return sines, cosines


def inverse_chord(wavenumber):
    chord = 2.0 * jnp.sin((math.pi / NPHI) * wavenumber.astype(F32))
    zero = wavenumber == 0
    return jnp.where(zero, 0.0, 1.0 / jnp.where(zero, 1.0, chord))


def cycle_mix(panel_orders, first_order, ord_count, cycle_span, cycle_weight):
    cell_angle = 2.0 * math.pi / NPHI
    start, stop = cycle_span[:, 0], cycle_span[:, 1]
    orders = first_order + jnp.arange(ord_count, dtype=jnp.int32)
    stop_sin, stop_cos = order_sines(first_order, ord_count, stop)
    start_sin, start_cos = order_sines(first_order, ord_count, start)
    pan_stop_sin, pan_stop_cos = sine_pair(panel_orders, stop)
    pan_start_sin, pan_start_cos = sine_pair(panel_orders, start)
    gap = panel_orders[:, None] - orders[None, :]
    total = panel_orders[:, None] + orders[None, :]
    gap_inv, sum_inv = inverse_chord(gap), inverse_chord(total)
    zeros = (gap == 0).astype(F32) + (total == 0).astype(F32)
    even = pan_stop_sin[:, None] * stop_cos[None] - pan_start_sin[:, None] * start_cos[None]
    odd = pan_stop_cos[:, None] * stop_sin[None] - pan_start_cos[:, None] * start_sin[None]
    width = (stop - start).astype(F32)
    mixed = (
        even * (sum_inv + gap_inv)[:, :, None]
        + odd * (sum_inv - gap_inv)[:, :, None]
        + zeros[:, :, None] * width[None, None, :]
    )
    return (0.5 * cell_angle) * cycle_weight[None, None, :] * mixed


def kernel(
    rows, cols, chunk,
    t_hbm, v_hbm, coef_ref, keep_ref, pick_ref, out_ref,
    tbuf, vbuf, vt, acc, own, half_send, half_recv, row_send, row_recv,
    pick_recv, tm, op_send, op_recv, fin_send, fin_recv,
    in_sem, half_ss, half_rs, row_ss, row_rs, pick_ss, pick_rs,
    tmz_ss, tmz_rs, tmp_ss, tmp_rs, op_ss, op_rs, fin_ss, fin_rs,
):
    r = lax.axis_index("row")
    c = lax.axis_index("col")
    groups = cols // 2
    core = c % 2
    group = c // 2
    partner = group * 2 + 1 - core
    ords, degs, cyc = tbuf.shape
    vecs = vbuf.shape[2]
    half = vecs // 2
    n_chunks = ords // chunk
    depth = chunk * degs

    loads = []
    for i in range(n_chunks):
        piece = pl.ds(i * chunk, chunk)
        loads.append((
            pltpu.make_async_copy(t_hbm.at[piece], tbuf.at[piece], in_sem.at[0, i]),
            pltpu.make_async_copy(v_hbm.at[piece], vbuf.at[piece], in_sem.at[1, i]),
        ))
        loads[-1][0].start()
        loads[-1][1].start()

    barrier = pltpu.get_barrier_semaphore()
    pl.semaphore_signal(barrier, inc=1, device_id=(r, partner), device_id_type=MESH)
    for s in range(1, rows):
        pl.semaphore_signal(barrier, inc=1, device_id=((r + s) % rows, c), device_id_type=MESH)
    for i in range(1, groups):
        pl.semaphore_signal(
            barrier, inc=1, device_id=(r, ((group + i) % groups) * 2 + core), device_id_type=MESH
        )
    pl.semaphore_wait(barrier, 1 + (rows - 1) + (groups - 1))

    def remote(src, dst, ss, rs, dev):
        copy = pltpu.make_async_remote_copy(
            src_ref=src, dst_ref=dst, send_sem=ss, recv_sem=rs, device_id=dev, device_id_type=MESH
        )
        copy.start()
        return copy

    picks = [
        remote(pick_ref.at[(r + s) % rows], pick_recv.at[s - 1], pick_ss.at[s - 1], pick_rs.at[s - 1],
               ((r + s) % rows, c))
        for s in range(1, rows)
    ]

    def scaled(panel, i):
        terms = []
        for o in range(chunk):
            index = i * chunk + o
            scale = jnp.broadcast_to(coef_ref[panel, pl.ds(index, 1), :], (16, cyc)).astype(BF16)
            block = tbuf[index].reshape(degs // 16, 16, cyc) * scale[None]
            terms.append(block.reshape(degs, cyc))
        return jnp.concatenate(terms, axis=0)

    def phase(panel, first):
        acc[...] = jnp.zeros_like(acc)
        if first:
            for i in range(n_chunks):
                loads[i][0].wait()
                loads[i][1].wait()
                span = slice(i * depth, (i + 1) * depth)
                block = vbuf[i * chunk:(i + 1) * chunk].reshape(depth, vecs)
                turned = block.T * jnp.broadcast_to(keep_ref[:, span], (16, depth)).astype(BF16)[:1]
                vt[:, span] = turned
                acc[...] += jnp.dot(turned, scaled(panel, i), preferred_element_type=F32)
        else:
            @pl.loop(0, n_chunks)
            def _(i):
                left = vt[:, pl.ds(pl.multiple_of(i * depth, depth), depth)]
                acc[...] += jnp.dot(left, scaled(panel, i), preferred_element_type=F32)

    mine = pl.ds(pl.multiple_of(core * half, half), half)
    other = pl.ds(pl.multiple_of((1 - core) * half, half), half)
    halves = []
    rowed = []

    def send_half(s):
        own[s] = acc[mine, :]
        half_send[s] = acc[other, :].astype(BF16)
        halves.append(remote(half_send.at[s], half_recv.at[s], half_ss.at[s], half_rs.at[s], (r, partner)))

    def send_row(s):
        halves[s].wait()
        row_send[s] = (own[s] + half_recv[s].astype(F32)).astype(BF16)
        rowed.append(remote(row_send.at[s], row_recv.at[s], row_ss.at[s], row_rs.at[s], ((r + s + 1) % rows, c)))

    later = []
    for s in range(rows):
        phase((r + s + 1) % rows, s == 0)
        send_half(s)
        if s == 0:
            for copy in picks:
                copy.wait()
            found = pick_ref[r].astype(F32)
            for q in range(rows - 1):
                found = found + pick_recv[q].astype(F32)
            tm[c] = found.astype(BF16)
            later = [
                remote(tm.at[c], tm.at[c], tmz_ss.at[i - 1], tmz_rs.at[i - 1],
                       (r, ((group + i) % groups) * 2 + core))
                for i in range(1, groups)
            ]
            later_core = [remote(tm.at[c], tm.at[c], tmp_ss.at[0], tmp_rs.at[0], (r, partner))]
        else:
            send_row(s - 1)
        if s == 1:
            for i in range(1, groups):
                later[i - 1].wait()
                came = ((group - i + groups) % groups) * 2 + core
                later_core.append(
                    remote(tm.at[came], tm.at[came], tmp_ss.at[i], tmp_rs.at[i], (r, partner))
                )
    for copy in later_core:
        copy.wait()
    halves[rows - 1].wait()
    summed = own[rows - 1] + half_recv[rows - 1].astype(F32)
    for s in range(rows - 1):
        rowed[s].wait()
        summed = summed + row_recv[s].astype(F32)
    summed = summed.astype(BF16)
    table = tm[...].reshape(cols * degs, cyc)
    product = lax.dot_general(table, summed, (((1,), (1,)), ((), ())), preferred_element_type=F32)
    op_send[...] = product.astype(BF16).reshape(groups, 2 * degs, half)
    sends = []
    for i in range(1, groups):
        to = (group + i) % groups
        sends.append(
            remote(op_send.at[to], op_recv.at[i - 1], op_ss.at[i - 1], op_rs.at[i - 1], (r, to * 2 + core))
        )
    total = op_send[group].astype(F32)
    for i in range(1, groups):
        sends[i - 1].wait()
        total = total + op_recv[i - 1].astype(F32)
    own[0, :2 * degs, :half] = total
    near = own[0, pl.ds(pl.multiple_of(core * degs, degs), degs), :half]
    far = own[0, pl.ds(pl.multiple_of((1 - core) * degs, degs), degs), :half]
    fin_send[...] = far.astype(BF16)
    last = remote(fin_send, fin_recv, fin_ss, fin_rs, (r, partner))
    out_ref[:, mine] = near.astype(BF16)
    last.wait()
    out_ref[:, other] = fin_recv[...]


def per_device(rows, cols, legendre, vectors, panel_orders, cycle_span, cycle_weight):
    ords, degs, cyc = legendre.shape
    vecs = vectors.shape[2]
    panels = panel_orders.shape[0]
    assert panels == rows
    first_order = lax.axis_index("row") * ords
    first_degree = lax.axis_index("col") * degs
    local_orders = first_order + jnp.arange(ords, dtype=jnp.int32)
    local_degrees = first_degree + jnp.arange(degs, dtype=jnp.int32)
    keep = (local_degrees[None, :] >= local_orders[:, None]).astype(F32).reshape(1, ords * degs)
    coef = cycle_mix(panel_orders, first_order, ords, cycle_span, cycle_weight)
    place = jnp.clip(panel_orders - first_order, 0, ords - 1)
    held = (panel_orders >= first_order) & (panel_orders < first_order + ords)
    held = held[:, None] & (local_degrees[None, :] >= panel_orders[:, None])
    picked = jnp.concatenate(
        [lax.dynamic_slice_in_dim(legendre, place[p], 1, 0) for p in range(panels)], axis=0
    )
    picked = jnp.where(held[:, :, None], picked, jnp.zeros((), BF16))

    groups, half = cols // 2, vecs // 2
    chunk = 8
    while ords % chunk or (chunk * degs) % 128:
        chunk *= 2
    dma = pltpu.SemaphoreType.DMA
    vmem = pl.BlockSpec(memory_space=pltpu.VMEM)
    hbm = pl.BlockSpec(memory_space=pl.ANY)
    return pl.pallas_call(
        functools.partial(kernel, rows, cols, chunk),
        out_shape=jax.ShapeDtypeStruct((degs, vecs), BF16),
        in_specs=[hbm, hbm, vmem, vmem, vmem],
        out_specs=vmem,
        scratch_shapes=[
            pltpu.VMEM((ords, degs, cyc), BF16),
            pltpu.VMEM((ords, degs, vecs), BF16),
            pltpu.VMEM((vecs, ords * degs), BF16),
            pltpu.VMEM((vecs, cyc), F32),
            pltpu.VMEM((rows, half, cyc), F32),
            pltpu.VMEM((rows, half, cyc), BF16),
            pltpu.VMEM((rows, half, cyc), BF16),
            pltpu.VMEM((rows - 1, half, cyc), BF16),
            pltpu.VMEM((rows - 1, half, cyc), BF16),
            pltpu.VMEM((rows - 1, degs, cyc), BF16),
            pltpu.VMEM((cols, degs, cyc), BF16),
            pltpu.VMEM((groups, 2 * degs, half), BF16),
            pltpu.VMEM((groups - 1, 2 * degs, half), BF16),
            pltpu.VMEM((degs, half), BF16),
            pltpu.VMEM((degs, half), BF16),
            dma((2, ords // chunk)),
            dma((rows,)), dma((rows,)),
            dma((rows - 1,)), dma((rows - 1,)),
            dma((rows - 1,)), dma((rows - 1,)),
            dma((groups - 1,)), dma((groups - 1,)),
            dma((groups,)), dma((groups,)),
            dma((groups - 1,)), dma((groups - 1,)),
            dma, dma,
        ],
        compiler_params=pltpu.CompilerParams(
            collective_id=0, has_side_effects=True, vmem_limit_bytes=60 * 1024 * 1024
        ),
    )(legendre, vectors, coef, keep, picked)


def solution(mesh):
    rows, cols = mesh.shape["row"], mesh.shape["col"]

    def body(*args):
        return per_device(rows, cols, *args)[:, None, :]

    in_specs = (P("row", "col", None), P("row", "col", None), P(), P(), P())
    return jax.shard_map(
        body, mesh=mesh, in_specs=in_specs, out_specs=P("col", "row", None), check_vma=False
    )
```

profile of v0, /device:TPU:0, one launch (start us, length us, event | category | flops | bytes accessed | tf_op | source)
XLA Modules:
  0.0 57.9 jit_solution(15921467461952854493)
XLA Ops:
  0.0 0.8 %fusion.46 = (s32[512,1]{0,1:T(1,128)S(1)}, s32[512,1]{0,1:T(1,128)S(1)}) fusion(s32[512,2]{0,1:T(2,128)} %param.8), kind=kLoop, calls=%fused_computation.98 | loop fusion | bytes 8192 | tf_op jit(solution)/shard_map/slice | solution.py:42
  0.8 0.2 fusion.31
  1.0 0.1 fusion.21
  1.1 0.1 fusion.19
  1.3 0.1 multiply_subtract_fusion
  1.4 0.9 %fusion.35 = (f32[4,512]{1,0:T(4,128)S(1)}, f32[4,512]{1,0:T(4,128)S(1)}, f32[4,512]{1,0:T(4,128)S(1)}, f32[4,512]{1,0:T(4,128)S(1)}) fusion(s32[512]{0:T(512)S(1)} %bitcast.22, s32[4]{0:T(128)} %param.7, s32[512]{0:T(512)S(1)} %bitcast.18), kind=kLoop, calls=%fused_computation.68 | loop fusion | flops 57344 | bytes 36880 | tf_op jit(solution)/shard_map/sin | solution.py:19
  2.3 0.8 %fusion.45 = (f32[4,128]{1,0:T(4,128)S(1)}, f32[4,128]{1,0:T(4,128)S(1)}, f32[4,128]{1,0:T(4,128)S(1)}) fusion(s32[128]{0:T(128)S(1)} %iota_add_fusion.1, s32[4]{0:T(128)} %param.7), kind=kLoop, calls=%fused_computation.88 | loop fusion | flops 10752 | bytes 6672 | tf_op jit(solution)/shard_map/add | solution.py:56
  3.1 0.7 %broadcast_multiply_fusion = f32[512]{0:T(512)S(1)} fusion(f32[512]{0:T(512)} %param.9), kind=kLoop, calls=%fused_computation.93 | loop fusion | flops 512 | bytes 4096 | tf_op jit(solution)/shard_map/mul | solution.py:60
  3.8 1.5 %add_multiply_fusion.coef_ref = f32[4,128,512]{2,1,0:T(8,128)} fusion(f32[512]{0:T(512)S(1)} %subtract_convert_fusion.1, f32[4,128]{1,0:T(4,128)S(1)} %get-tuple-element.29, f32[4,128]{1,0:T(4,128)S(1)} %get-tuple-element.28, f32[128,512]{1,0:T(8,128)S(1)} %bitcast.12, f32[4,512]{1,0:T(4,128)S(1)} %get-tuple-element.34, f32[128,512]{1,0:T(8,128)S(1)} %bitcast.13, ...), kind=kLoop, calls=%fused_computation | loop fusion | flops 3145728 | bytes 2140160 | tf_op jit(solution)/shard_map/mul | solution.py:60
  5.4 0.7 %subtract_clamp_fusion = s32[4]{0:T(128)S(1)} fusion(s32[4]{0:T(128)} %param.7, s32[]{:T(128)S(6)} %mul.467), kind=kLoop, calls=%fused_computation.94 | loop fusion | flops 8 | bytes 36 | tf_op jit(solution)/shard_map/jit(clip)/min | solution.py:225
  6.0 0.6 %fusion.47 = (s32[1]{0:T(128)}, s32[1]{0:T(128)}, s32[1]{0:T(128)}, s32[1]{0:T(128)}) fusion(s32[4]{0:T(128)S(1)} %subtract_clamp_fusion), kind=kLoop, calls=%fused_computation.99 | loop fusion | bytes 32 | tf_op jit(solution)/shard_map/slice | solution.py:229
  14.1 1.0 %constant_dynamic-slice_fusion.3 = (bf16[1,64,512]{2,1,0:T(8,128)(2,1)S(1)}, bf16[1,64,512]{2,1,0:T(8,128)(2,1)S(1)}, bf16[1,64,512]{2,1,0:T(8,128)(2,1)S(1)}, bf16[1,64,512]{2,1,0:T(8,128)(2,1)S(1)}) fusion(bf16[128,64,512]{2,1,0:T(8,128)(2,1)} %t_hbm.1, s32[]{:T(128)S(6)} %select_n.140, s32[]{:T(128)S(6)} %select_n.142, s32[]{:T(128)S(6)} %select_n.141, ...), kind=kLoop, calls=%fused_computation.92 | loop fusion | bytes 524304 | tf_op jit(solution)/shard_map/dynamic_slice | solution.py:229
  15.1 0.7 %compare_and_fusion.1 = pred[4]{0:T(512)(128)(4,1)S(1)} fusion(s32[4]{0:T(128)} %param.7, s32[]{:T(128)S(6)} %add.211, s32[]{:T(128)S(6)} %mul.467), kind=kLoop, calls=%fused_computation.86 | loop fusion | flops 12 | bytes 28 | tf_op jit(solution)/shard_map/and | solution.py:226
  15.8 0.7 %compare_and_fusion = pred[4,64]{1,0:T(4,128)(4,1)S(1)} fusion(s32[64]{0:T(128)S(1)} %iota_add_fusion, s32[4]{0:T(128)} %param.7, pred[4]{0:T(512)(128)(4,1)S(1)} %compare_and_fusion.1), kind=kLoop, calls=%fused_computation.85 | loop fusion | flops 512 | bytes 532 | tf_op jit(solution)/shard_map/and | solution.py:227
  16.5 0.8 %maximum_select_fusion.pick_ref = bf16[4,64,512]{2,1,0:T(8,128)(2,1)} fusion(bf16[1,64,512]{2,1,0:T(8,128)(2,1)S(1)} %get-tuple-element.8, bf16[1,64,512]{2,1,0:T(8,128)(2,1)S(1)} %get-tuple-element.6, bf16[1,64,512]{2,1,0:T(8,128)(2,1)S(1)} %get-tuple-element.7, bf16[1,64,512]{2,1,0:T(8,128)(2,1)S(1)} %get-tuple-element.5, pred[4,64]{1,0:T(4,128)(4,1)S(1)} %compare_and_fusion), kind=kLoop, calls=%fused_computation.1 | loop fusion | flops 524288 | bytes 524544 | tf_op jit(solution)/shard_map/jit(_where)/select_n | solution.py:231
  17.4 0.1 compare_convert_fusion
  17.4 0.7 %reshape.762.keep_ref = f32[1,8192]{1,0:T(1,128)} reshape(f32[128,64]{1,0:T(8,128)S(1)} %compare_convert_fusion) | data formatting | bytes 65536 | tf_op jit(solution)/shard_map/convert_element_type | solution.py:223
  18.2 38.4 %shard_map.55 = bf16[64,256]{1,0:T(8,128)(2,1)} custom-call(bf16[128,64,512]{2,1,0:T(8,128)(2,1)} %t_hbm.1, bf16[128,64,256]{2,1,0:T(8,128)(2,1)} %v_hbm.1, f32[4,128,512]{2,1,0:T(8,128)} %add_multiply_fusion.coef_ref, f32[1,8192]{1,0:T(1,128)} %reshape.762.keep_ref, bf16[4,64,512]{2,1,0:T(8,128)(2,1)} %maximum_select_fusion.pick_ref), custom_call_target="tpu_custom_call" | custom-call | tf_op jit(solution)/shard_map/pallas_call | solution.py:240
  56.6 1.4 %copy.7 = bf16[64,1,256]{2,0,1:T(8,128)(2,1)} copy(bf16[64,1,256]{2,0,1:T(8,128)(2,1)} %bitcast.15) | data formatting | bytes 65536
  (4 shorter events, 0.0 us)
where the time goes:
time: 58.4 us; the launch traced here: 57.9 us
  Pallas kernels  38.4 us (66%)
  between operations  7.58 us (13%)
  other arithmetic  7.5 us (13%)
  local copies, waits for them, and re-layouts  4.46 us (8%)
    pallas_call x1, Pallas kernels, per_device(): pl.pallas_call(functools.partial(kernel, rows, cols, chunk), out_shape=ja...  38.4 us
    mul x2, other arithmetic, cycle_mix(): return 0.5 * cell_angle * cycle_weight[None, None, :] * mixed  2.23 us
    unnamed x1, local copies, waits for them, and re-layouts  1.38 us

commit v1 on v0

--- a/solution.py
+++ b/solution.py
@@ -15,55 +15,60 @@
 
 
 def sine_pair(orders, cells):
-    angle = (2.0 * math.pi / NPHI) * (orders[:, None] * cells[None, :] % NPHI).astype(F32)
+    angle = (2.0 * math.pi / NPHI) * ((orders * cells) & (NPHI - 1)).astype(F32)
     return jnp.sin(angle), jnp.cos(angle)
 
 
-def order_sines(first_order, ord_count, cells):
+def cycle_mix(order_of, panels, first_order, span, weight, coef_ref):
+    ords, cyc = coef_ref.shape[1:]
     step = 16
-    high_sin, high_cos = sine_pair(first_order + step * jnp.arange(ord_count // step, dtype=jnp.int32), cells)
-    low_sin, low_cos = sine_pair(jnp.arange(step, dtype=jnp.int32), cells)
-    high_sin, high_cos = high_sin[:, None], high_cos[:, None]
-    low_sin, low_cos = low_sin[None], low_cos[None]
-    shape = (ord_count, cells.shape[0])
-    sines = (high_sin * low_cos + high_cos * low_sin).reshape(shape)
-    cosines = (high_cos * low_cos - high_sin * low_sin).reshape(shape)
-    return sines, cosines
-
-
-def inverse_chord(wavenumber):
-    chord = 2.0 * jnp.sin((math.pi / NPHI) * wavenumber.astype(F32))
-    zero = wavenumber == 0
-    return jnp.where(zero, 0.0, 1.0 / jnp.where(zero, 1.0, chord))
-
-
-def cycle_mix(panel_orders, first_order, ord_count, cycle_span, cycle_weight):
     cell_angle = 2.0 * math.pi / NPHI
-    start, stop = cycle_span[:, 0], cycle_span[:, 1]
-    orders = first_order + jnp.arange(ord_count, dtype=jnp.int32)
-    stop_sin, stop_cos = order_sines(first_order, ord_count, stop)
-    start_sin, start_cos = order_sines(first_order, ord_count, start)
-    pan_stop_sin, pan_stop_cos = sine_pair(panel_orders, stop)
-    pan_start_sin, pan_start_cos = sine_pair(panel_orders, start)
-    gap = panel_orders[:, None] - orders[None, :]
-    total = panel_orders[:, None] + orders[None, :]
-    gap_inv, sum_inv = inverse_chord(gap), inverse_chord(total)
-    zeros = (gap == 0).astype(F32) + (total == 0).astype(F32)
-    even = pan_stop_sin[:, None] * stop_cos[None] - pan_start_sin[:, None] * start_cos[None]
-    odd = pan_stop_cos[:, None] * stop_sin[None] - pan_start_cos[:, None] * start_sin[None]
-    width = (stop - start).astype(F32)
-    mixed = (
-        even * (sum_inv + gap_inv)[:, :, None]
-        + odd * (sum_inv - gap_inv)[:, :, None]
-        + zeros[:, :, None] * width[None, None, :]
-    )
-    return (0.5 * cell_angle) * cycle_weight[None, None, :] * mixed
+    start, stop = span[0:1, :], span[1:2, :]
+    scale = (0.5 * cell_angle) * weight
+    width = scale * (stop - start).astype(F32)
+    low = lax.broadcasted_iota(jnp.int32, (step, cyc), 0)
+    high_count = ords // step
+    high = first_order + step * lax.broadcasted_iota(jnp.int32, (high_count, cyc), 0)
+    low_stop, low_start = sine_pair(low, stop), sine_pair(low, start)
+    high_stop, high_start = sine_pair(high, stop), sine_pair(high, start)
+    ident = lax.broadcasted_iota(jnp.int32, (panels, cyc), 0)
+    pan = jnp.zeros((panels, cyc), jnp.int32)
+    for p in range(panels):
+        pan = jnp.where(ident == p, order_of[p], pan)
+    pan_stop = [scale * x for x in sine_pair(pan, stop)]
+    pan_start = [scale * x for x in sine_pair(pan, start)]
+    lane = lax.broadcasted_iota(jnp.int32, (ords, 128), 1)
+    order = first_order + lax.broadcasted_iota(jnp.int32, (ords, 128), 0)
+    wave = jnp.ones((ords, 128), jnp.int32)
+    for p in range(panels):
+        wave = jnp.where(lane == 2 * p, order_of[p] - order, wave)
+        wave = jnp.where(lane == 2 * p + 1, order_of[p] + order, wave)
+    zero = wave == 0
+    chord = 2.0 * jnp.sin((math.pi / NPHI) * wave.astype(F32))
+    inverse = jnp.where(zero, 0.0, 1.0 / jnp.where(zero, 1.0, chord))
+    zeros = zero.astype(F32)
+    for a in range(high_count):
+        rows = slice(a * step, (a + 1) * step)
+
+        def turned(high_pair, low_pair):
+            hs, hc = high_pair[0][a:a + 1], high_pair[1][a:a + 1]
+            return hs * low_pair[1] + hc * low_pair[0], hc * low_pair[1] - hs * low_pair[0]
+
+        stop_sin, stop_cos = turned(high_stop, low_stop)
+        start_sin, start_cos = turned(high_start, low_start)
+        for p in range(panels):
+            one = slice(p, p + 1)
+            even = pan_stop[0][one] * stop_cos - pan_start[0][one] * start_cos
+            odd = pan_stop[1][one] * stop_sin - pan_start[1][one] * start_sin
+            gap, total = inverse[rows, 2 * p:2 * p + 1], inverse[rows, 2 * p + 1:2 * p + 2]
+            flat = zeros[rows, 2 * p:2 * p + 1] + zeros[rows, 2 * p + 1:2 * p + 2]
+            coef_ref[p, rows, :] = even * (total + gap) + odd * (total - gap) + flat * width
 
 
 def kernel(
     rows, cols, chunk,
-    t_hbm, v_hbm, coef_ref, keep_ref, pick_ref, out_ref,
-    tbuf, vbuf, vt, acc, own, half_send, half_recv, row_send, row_recv,
+    t_hbm, v_hbm, order_ref, span_ref, weight_ref, out_ref,
+    coef_ref, pick_ref, tbuf, vbuf, vt, acc, own, half_send, half_recv, row_send, row_recv,
     pick_recv, tm, op_send, op_recv, fin_send, fin_recv,
     in_sem, half_ss, half_rs, row_ss, row_rs, pick_ss, pick_rs,
     tmz_ss, tmz_rs, tmp_ss, tmp_rs, op_ss, op_rs, fin_ss, fin_rs,
@@ -107,11 +112,24 @@
         copy.start()
         return copy
 
-    picks = [
-        remote(pick_ref.at[(r + s) % rows], pick_recv.at[s - 1], pick_ss.at[s - 1], pick_rs.at[s - 1],
-               ((r + s) % rows, c))
-        for s in range(1, rows)
-    ]
+    panels = rows
+    first_order, first_degree = r * ords, c * degs
+    order_of = [order_ref[p] for p in range(panels)]
+    cycle_mix(order_of, panels, first_order, span_ref[...], weight_ref[...], coef_ref)
+
+    def kept(i):
+        index = i * depth + lax.broadcasted_iota(jnp.int32, (16, depth), 1)
+        shift = degs.bit_length() - 1
+        order = first_order + lax.shift_right_logical(index, shift)
+        degree = first_degree + (index & (degs - 1))
+        return jnp.where(degree >= order, 1.0, 0.0).astype(BF16)[:1]
+
+    def pick(p):
+        place = jnp.clip(order_of[p] - first_order, 0, ords - 1)
+        held = (order_of[p] >= first_order) & (order_of[p] < first_order + ords)
+        degree = first_degree + lax.broadcasted_iota(jnp.int32, (degs, cyc), 0)
+        keep = (degree >= order_of[p]) & held
+        pick_ref[p] = jnp.where(keep, tbuf[place].astype(F32), 0.0).astype(BF16)
 
     def scaled(panel, i):
         terms = []
@@ -130,7 +148,7 @@
                 loads[i][1].wait()
                 span = slice(i * depth, (i + 1) * depth)
                 block = vbuf[i * chunk:(i + 1) * chunk].reshape(depth, vecs)
-                turned = block.T * jnp.broadcast_to(keep_ref[:, span], (16, depth)).astype(BF16)[:1]
+                turned = block.T * kept(i)
                 vt[:, span] = turned
                 acc[...] += jnp.dot(turned, scaled(panel, i), preferred_element_type=F32)
         else:
@@ -154,11 +172,20 @@
         row_send[s] = (own[s] + half_recv[s].astype(F32)).astype(BF16)
         rowed.append(remote(row_send.at[s], row_recv.at[s], row_ss.at[s], row_rs.at[s], ((r + s + 1) % rows, c)))
 
-    later = []
     for s in range(rows):
         phase((r + s + 1) % rows, s == 0)
         send_half(s)
         if s == 0:
+            for p in range(panels):
+                pick(p)
+            picks = [
+                remote(pick_ref.at[(r + q) % rows], pick_recv.at[q - 1], pick_ss.at[q - 1],
+                       pick_rs.at[q - 1], ((r + q) % rows, c))
+                for q in range(1, rows)
+            ]
+        else:
+            send_row(s - 1)
+        if s == 1:
             for copy in picks:
                 copy.wait()
             found = pick_ref[r].astype(F32)
@@ -171,9 +198,7 @@
                 for i in range(1, groups)
             ]
             later_core = [remote(tm.at[c], tm.at[c], tmp_ss.at[0], tmp_rs.at[0], (r, partner))]
-        else:
-            send_row(s - 1)
-        if s == 1:
+        if s == 2:
             for i in range(1, groups):
                 later[i - 1].wait()
                 came = ((group - i + groups) % groups) * 2 + core
@@ -216,20 +241,6 @@
     vecs = vectors.shape[2]
     panels = panel_orders.shape[0]
     assert panels == rows
-    first_order = lax.axis_index("row") * ords
-    first_degree = lax.axis_index("col") * degs
-    local_orders = first_order + jnp.arange(ords, dtype=jnp.int32)
-    local_degrees = first_degree + jnp.arange(degs, dtype=jnp.int32)
-    keep = (local_degrees[None, :] >= local_orders[:, None]).astype(F32).reshape(1, ords * degs)
-    coef = cycle_mix(panel_orders, first_order, ords, cycle_span, cycle_weight)
-    place = jnp.clip(panel_orders - first_order, 0, ords - 1)
-    held = (panel_orders >= first_order) & (panel_orders < first_order + ords)
-    held = held[:, None] & (local_degrees[None, :] >= panel_orders[:, None])
-    picked = jnp.concatenate(
-        [lax.dynamic_slice_in_dim(legendre, place[p], 1, 0) for p in range(panels)], axis=0
-    )
-    picked = jnp.where(held[:, :, None], picked, jnp.zeros((), BF16))
-
     groups, half = cols // 2, vecs // 2
     chunk = 8
     while ords % chunk or (chunk * degs) % 128:
@@ -240,9 +251,11 @@
     return pl.pallas_call(
         functools.partial(kernel, rows, cols, chunk),
         out_shape=jax.ShapeDtypeStruct((degs, vecs), BF16),
-        in_specs=[hbm, hbm, vmem, vmem, vmem],
+        in_specs=[hbm, hbm, pl.BlockSpec(memory_space=pltpu.SMEM), vmem, vmem],
         out_specs=vmem,
         scratch_shapes=[
+            pltpu.VMEM((panels, ords, cyc), F32),
+            pltpu.VMEM((panels, degs, cyc), BF16),
             pltpu.VMEM((ords, degs, cyc), BF16),
             pltpu.VMEM((ords, degs, vecs), BF16),
             pltpu.VMEM((vecs, ords * degs), BF16),
@@ -270,7 +283,7 @@
         compiler_params=pltpu.CompilerParams(
             collective_id=0, has_side_effects=True, vmem_limit_bytes=60 * 1024 * 1024
         ),
-    )(legendre, vectors, coef, keep, picked)
+    )(legendre, vectors, panel_orders, cycle_span.T, cycle_weight[None, :])
 
 
 def solution(mesh):

time: 58.4 us -> 40.5 us (0.69)
  between operations: 7.58 us -> 0.01 us
  other arithmetic: 7.5 us -> 0 us
  local copies, waits for them, and re-layouts: 4.46 us -> 1.38 us
    mul x2 -> x0, other arithmetic: 2.23 us -> none  [cycle_mix(): return 0.5 * cell_angle * cycle_weight[None, None, :] * mixed]
    and x2 -> x0, other arithmetic: 1.39 us -> none  [the longest x1 0.73 us: per_device(): held = held[:, None] & (local_degrees[None, :] >= panel_orders[:, None])]
    slice x2 -> x0, local copies, waits for them, and re-layouts: 1.39 us -> none  [the longest x1 0.77 us: cycle_mix(): start, stop = (cycle_span[:, 0], cycle_span[:, 1])]
    dynamic_slice x1 -> x0, local copies, waits for them, and re-layouts: 0.98 us -> none  [per_device(): lax.dynamic_slice_in_dim(legendre, place[p], 1, 0)]
    sin x1 -> x0, other arithmetic: 0.87 us -> none  [sine_pair(): return (jnp.sin(angle), jnp.cos(angle))]
    select_n x1 -> x0, other arithmetic: 0.82 us -> none  [per_device(): picked = jnp.where(held[:, :, None], picked, jnp.zeros((), BF16))]
    add x4 -> x0, other arithmetic: 0.79 us -> none  [the longest x1 0.78 us: cycle_mix(): sum_inv + gap_inv]
    convert_element_type x1 -> x0, local copies, waits for them, and re-layouts: 0.71 us -> none  [per_device(): (local_degrees[None, :] >= local_orders[:, None]).astype(F32)]
where the time goes in v1:
time: 40.5 us; the launch traced here: 40.3 us
  Pallas kernels  38.9 us (96%)
  local copies, waits for them, and re-layouts  1.38 us (3%)
    pallas_call x1, Pallas kernels, per_device(): pl.pallas_call(functools.partial(kernel, rows, cols, chunk), out_shape=ja...  38.9 us
    unnamed x1, local copies, waits for them, and re-layouts  1.38 us

profile of v1, /device:TPU:0, one launch (start us, length us, event | category | flops | bytes accessed | tf_op | source)
XLA Modules:
  0.0 40.3 jit_solution(11376865062367409699)
XLA Ops:
  0.0 38.9 %shard_map.55 = bf16[64,256]{1,0:T(8,128)(2,1)} custom-call(bf16[128,64,512]{2,1,0:T(8,128)(2,1)} %t_hbm.1, bf16[128,64,256]{2,1,0:T(8,128)(2,1)} %v_hbm.1, s32[4]{0:T(128)} %order_ref.1, s32[2,512]{1,0:T(2,128)} %bitcast.4, f32[1,512]{1,0:T(1,128)} %bitcast.5), custom_call_target="tpu_custom_call" | custom-call | tf_op jit(solution)/shard_map/pallas_call | solution.py:251
  38.9 1.4 %copy.7 = bf16[64,1,256]{2,0,1:T(8,128)(2,1)} copy(bf16[64,1,256]{2,0,1:T(8,128)(2,1)} %bitcast.3) | data formatting | bytes 65536

commit v2 on v1

--- a/solution.py
+++ b/solution.py
@@ -131,41 +131,51 @@
         keep = (degree >= order_of[p]) & held
         pick_ref[p] = jnp.where(keep, tbuf[place].astype(F32), 0.0).astype(BF16)
 
-    def scaled(panel, i):
+    def scaled(panel, start, count, span):
+        width = cyc if span is None else cyc // 2
+        span = slice(None) if span is None else span
         terms = []
-        for o in range(chunk):
-            index = i * chunk + o
-            scale = jnp.broadcast_to(coef_ref[panel, pl.ds(index, 1), :], (16, cyc)).astype(BF16)
-            block = tbuf[index].reshape(degs // 16, 16, cyc) * scale[None]
-            terms.append(block.reshape(degs, cyc))
+        for o in range(count):
+            index = start + o
+            scale = jnp.broadcast_to(coef_ref[panel, pl.ds(index, 1), span], (16, width)).astype(BF16)
+            block = tbuf[index, :, span].reshape(degs // 16, 16, width) * scale[None]
+            terms.append(block.reshape(degs, width))
         return jnp.concatenate(terms, axis=0)
 
-    def phase(panel, first):
+    def first_phase(panel):
         acc[...] = jnp.zeros_like(acc)
-        if first:
-            for i in range(n_chunks):
-                loads[i][0].wait()
-                loads[i][1].wait()
-                span = slice(i * depth, (i + 1) * depth)
-                block = vbuf[i * chunk:(i + 1) * chunk].reshape(depth, vecs)
-                turned = block.T * kept(i)
-                vt[:, span] = turned
-                acc[...] += jnp.dot(turned, scaled(panel, i), preferred_element_type=F32)
-        else:
-            @pl.loop(0, n_chunks)
-            def _(i):
-                left = vt[:, pl.ds(pl.multiple_of(i * depth, depth), depth)]
-                acc[...] += jnp.dot(left, scaled(panel, i), preferred_element_type=F32)
+        for i in range(n_chunks):
+            loads[i][0].wait()
+            loads[i][1].wait()
+            span = slice(i * depth, (i + 1) * depth)
+            block = vbuf[i * chunk:(i + 1) * chunk].reshape(depth, vecs)
+            turned = block.T * kept(i)
+            vt[:, span] = turned
+            acc[...] += jnp.dot(turned, scaled(panel, i * chunk, chunk, None), preferred_element_type=F32)
+
+    def half_phase(panel, span):
+        acc[:, span] = jnp.zeros((vecs, cyc // 2), F32)
+        merge = 4 if ords % (4 * chunk) == 0 else 1
+        large, long = merge * chunk, merge * depth
+
+        @pl.loop(0, ords // large)
+        def _(i):
+            left = vt[:, pl.ds(pl.multiple_of(i * long, long), long)]
+            acc[:, span] += jnp.dot(left, scaled(panel, i * large, large, span), preferred_element_type=F32)
 
     mine = pl.ds(pl.multiple_of(core * half, half), half)
     other = pl.ds(pl.multiple_of((1 - core) * half, half), half)
     halves = []
     rowed = []
 
-    def send_half(s):
-        own[s] = acc[mine, :]
-        half_send[s] = acc[other, :].astype(BF16)
-        halves.append(remote(half_send.at[s], half_recv.at[s], half_ss.at[s], half_rs.at[s], (r, partner)))
+    spans = (slice(0, cyc // 2), slice(cyc // 2, cyc))
+
+    def send_half(s, span, sem):
+        own[s, :, span] = acc[mine, span]
+        half_send[s, :, span] = acc[other, span].astype(BF16)
+        halves.append(
+            remote(half_send.at[s, :, span], half_recv.at[s, :, span], half_ss.at[sem], half_rs.at[sem], (r, partner))
+        )
 
     def send_row(s):
         halves[s].wait()
@@ -173,9 +183,10 @@
         rowed.append(remote(row_send.at[s], row_recv.at[s], row_ss.at[s], row_rs.at[s], ((r + s + 1) % rows, c)))
 
     for s in range(rows):
-        phase((r + s + 1) % rows, s == 0)
-        send_half(s)
+        panel = (r + s + 1) % rows
         if s == 0:
+            first_phase(panel)
+            send_half(0, slice(0, cyc), 0)
             for p in range(panels):
                 pick(p)
             picks = [
@@ -183,8 +194,11 @@
                        pick_rs.at[q - 1], ((r + q) % rows, c))
                 for q in range(1, rows)
             ]
-        else:
-            send_row(s - 1)
+            continue
+        half_phase(panel, spans[0])
+        send_row(s - 1)
+        if s == rows - 1:
+            send_half(s, spans[0], s)
         if s == 1:
             for copy in picks:
                 copy.wait()
@@ -198,6 +212,11 @@
                 for i in range(1, groups)
             ]
             later_core = [remote(tm.at[c], tm.at[c], tmp_ss.at[0], tmp_rs.at[0], (r, partner))]
+        half_phase(panel, spans[1])
+        if s < rows - 1:
+            send_half(s, slice(0, cyc), s)
+        else:
+            send_half(s, spans[1], s + 1)
         if s == 2:
             for i in range(1, groups):
                 later[i - 1].wait()
@@ -208,6 +227,7 @@
     for copy in later_core:
         copy.wait()
     halves[rows - 1].wait()
+    halves[rows].wait()
     summed = own[rows - 1] + half_recv[rows - 1].astype(F32)
     for s in range(rows - 1):
         rowed[s].wait()
@@ -272,7 +292,7 @@
             pltpu.VMEM((degs, half), BF16),
             pltpu.VMEM((degs, half), BF16),
             dma((2, ords // chunk)),
-            dma((rows,)), dma((rows,)),
+            dma((rows + 1,)), dma((rows + 1,)),
             dma((rows - 1,)), dma((rows - 1,)),
             dma((rows - 1,)), dma((rows - 1,)),
             dma((groups - 1,)), dma((groups - 1,)),

time: 40.5 us -> 36.4 us (0.90)
  Pallas kernels: 38.9 us -> 34.8 us
    pallas_call x1, Pallas kernels: 38.9 us -> 34.8 us  [per_device(): pl.pallas_call(functools.partial(kernel, rows, cols, chunk), out_shape=ja...]
where the time goes in v2:
time: 36.4 us; the launch traced here: 36.2 us
  Pallas kernels  34.8 us (96%)
  local copies, waits for them, and re-layouts  1.38 us (4%)
    pallas_call x1, Pallas kernels, per_device(): pl.pallas_call(functools.partial(kernel, rows, cols, chunk), out_shape=ja...  34.8 us
    unnamed x1, local copies, waits for them, and re-layouts  1.38 us

profile of v2, /device:TPU:0, one launch (start us, length us, event | category | flops | bytes accessed | tf_op | source)
XLA Modules:
  0.0 36.2 jit_solution(10984568833460357565)
XLA Ops:
  0.0 34.8 %shard_map.55 = bf16[64,256]{1,0:T(8,128)(2,1)} custom-call(bf16[128,64,512]{2,1,0:T(8,128)(2,1)} %t_hbm.1, bf16[128,64,256]{2,1,0:T(8,128)(2,1)} %v_hbm.1, s32[4]{0:T(128)} %order_ref.1, s32[2,512]{1,0:T(2,128)} %bitcast.4, f32[1,512]{1,0:T(1,128)} %bitcast.5), custom_call_target="tpu_custom_call" | custom-call | tf_op jit(solution)/shard_map/pallas_call | solution.py:271
  34.8 1.4 %copy.7 = bf16[64,1,256]{2,0,1:T(8,128)(2,1)} copy(bf16[64,1,256]{2,0,1:T(8,128)(2,1)} %bitcast.3) | data formatting | bytes 65536

commit v3 on v2

--- a/solution.py
+++ b/solution.py
@@ -69,9 +69,9 @@
     rows, cols, chunk,
     t_hbm, v_hbm, order_ref, span_ref, weight_ref, out_ref,
     coef_ref, pick_ref, tbuf, vbuf, vt, acc, own, half_send, half_recv, row_send, row_recv,
-    pick_recv, tm, op_send, op_recv, fin_send, fin_recv,
+    pick_recv, tm, op_send, op_recv,
     in_sem, half_ss, half_rs, row_ss, row_rs, pick_ss, pick_rs,
-    tmz_ss, tmz_rs, tmp_ss, tmp_rs, op_ss, op_rs, fin_ss, fin_rs,
+    tmz_ss, tmz_rs, tmp_ss, tmp_rs, op_ss, op_rs,
 ):
     r = lax.axis_index("row")
     c = lax.axis_index("col")
@@ -96,14 +96,10 @@
         loads[-1][1].start()
 
     barrier = pltpu.get_barrier_semaphore()
-    pl.semaphore_signal(barrier, inc=1, device_id=(r, partner), device_id_type=MESH)
     for s in range(1, rows):
         pl.semaphore_signal(barrier, inc=1, device_id=((r + s) % rows, c), device_id_type=MESH)
-    for i in range(1, groups):
-        pl.semaphore_signal(
-            barrier, inc=1, device_id=(r, ((group + i) % groups) * 2 + core), device_id_type=MESH
-        )
-    pl.semaphore_wait(barrier, 1 + (rows - 1) + (groups - 1))
+    for i in range(1, cols):
+        pl.semaphore_signal(barrier, inc=1, device_id=(r, (c + i) % cols), device_id_type=MESH)
 
     def remote(src, dst, ss, rs, dev):
         copy = pltpu.make_async_remote_copy(
@@ -186,6 +182,7 @@
         panel = (r + s + 1) % rows
         if s == 0:
             first_phase(panel)
+            pl.semaphore_wait(barrier, (rows - 1) + (cols - 1))
             send_half(0, slice(0, cyc), 0)
             for p in range(panels):
                 pick(p)
@@ -235,25 +232,21 @@
     summed = summed.astype(BF16)
     table = tm[...].reshape(cols * degs, cyc)
     product = lax.dot_general(table, summed, (((1,), (1,)), ((), ())), preferred_element_type=F32)
-    op_send[...] = product.astype(BF16).reshape(groups, 2 * degs, half)
+    op_send[...] = product.astype(BF16).reshape(cols, degs, half)
     sends = []
-    for i in range(1, groups):
-        to = (group + i) % groups
-        sends.append(
-            remote(op_send.at[to], op_recv.at[i - 1], op_ss.at[i - 1], op_rs.at[i - 1], (r, to * 2 + core))
-        )
-    total = op_send[group].astype(F32)
-    for i in range(1, groups):
+    for i in range(1, cols):
+        to = (c + i) % cols
+        sends.append(remote(op_send.at[to], op_recv.at[i - 1], op_ss.at[i - 1], op_rs.at[i - 1], (r, to)))
+    near = op_send[c].astype(F32)
+    far = jnp.zeros((degs, half), F32)
+    for i in range(1, cols):
         sends[i - 1].wait()
-        total = total + op_recv[i - 1].astype(F32)
-    own[0, :2 * degs, :half] = total
-    near = own[0, pl.ds(pl.multiple_of(core * degs, degs), degs), :half]
-    far = own[0, pl.ds(pl.multiple_of((1 - core) * degs, degs), degs), :half]
-    fin_send[...] = far.astype(BF16)
-    last = remote(fin_send, fin_recv, fin_ss, fin_rs, (r, partner))
+        if i % 2:
+            far = far + op_recv[i - 1].astype(F32)
+        else:
+            near = near + op_recv[i - 1].astype(F32)
     out_ref[:, mine] = near.astype(BF16)
-    last.wait()
-    out_ref[:, other] = fin_recv[...]
+    out_ref[:, other] = far.astype(BF16)
 
 
 def per_device(rows, cols, legendre, vectors, panel_orders, cycle_span, cycle_weight):
@@ -287,18 +280,15 @@
             pltpu.VMEM((rows - 1, half, cyc), BF16),
             pltpu.VMEM((rows - 1, degs, cyc), BF16),
             pltpu.VMEM((cols, degs, cyc), BF16),
-            pltpu.VMEM((groups, 2 * degs, half), BF16),
-            pltpu.VMEM((groups - 1, 2 * degs, half), BF16),
-            pltpu.VMEM((degs, half), BF16),
-            pltpu.VMEM((degs, half), BF16),
+            pltpu.VMEM((cols, degs, half), BF16),
+            pltpu.VMEM((cols - 1, degs, half), BF16),
             dma((2, ords // chunk)),
             dma((rows + 1,)), dma((rows + 1,)),
             dma((rows - 1,)), dma((rows - 1,)),
             dma((rows - 1,)), dma((rows - 1,)),
             dma((groups - 1,)), dma((groups - 1,)),
             dma((groups,)), dma((groups,)),
-            dma((groups - 1,)), dma((groups - 1,)),
-            dma, dma,
+            dma((cols - 1,)), dma((cols - 1,)),
         ],
         compiler_params=pltpu.CompilerParams(
             collective_id=0, has_side_effects=True, vmem_limit_bytes=60 * 1024 * 1024

time: 36.4 us -> 33.9 us (0.931)
  Pallas kernels: 34.8 us -> 32.4 us
    pallas_call x1, Pallas kernels: 34.8 us -> 32.4 us  [per_device(): pl.pallas_call(functools.partial(kernel, rows, cols, chunk), out_shape=ja...]
where the time goes in v3:
time: 33.9 us; the launch traced here: 33.7 us
  Pallas kernels  32.4 us (96%)
  local copies, waits for them, and re-layouts  1.38 us (4%)
    pallas_call x1, Pallas kernels, per_device(): pl.pallas_call(functools.partial(kernel, rows, cols, chunk), out_shape=ja...  32.4 us
    unnamed x1, local copies, waits for them, and re-layouts  1.38 us

profile of v3, /device:TPU:0, one launch (start us, length us, event | category | flops | bytes accessed | tf_op | source)
XLA Modules:
  0.0 33.7 jit_solution(15850256959407779305)
XLA Ops:
  0.0 32.4 %shard_map.55 = bf16[64,256]{1,0:T(8,128)(2,1)} custom-call(bf16[128,64,512]{2,1,0:T(8,128)(2,1)} %t_hbm.1, bf16[128,64,256]{2,1,0:T(8,128)(2,1)} %v_hbm.1, s32[4]{0:T(128)} %order_ref.1, s32[2,512]{1,0:T(2,128)} %bitcast.4, f32[1,512]{1,0:T(1,128)} %bitcast.5), custom_call_target="tpu_custom_call" | custom-call | tf_op jit(solution)/shard_map/pallas_call | solution.py:264
  32.4 1.4 %copy.7 = bf16[64,1,256]{2,0,1:T(8,128)(2,1)} copy(bf16[64,1,256]{2,0,1:T(8,128)(2,1)} %bitcast.3) | data formatting | bytes 65536

commit v4 on v3

--- a/solution.py
+++ b/solution.py
@@ -151,7 +151,7 @@
 
     def half_phase(panel, span):
         acc[:, span] = jnp.zeros((vecs, cyc // 2), F32)
-        merge = 4 if ords % (4 * chunk) == 0 else 1
+        merge = 8 if ords % (8 * chunk) == 0 else 1
         large, long = merge * chunk, merge * depth
 
         @pl.loop(0, ords // large)
@@ -167,11 +167,11 @@
     spans = (slice(0, cyc // 2), slice(cyc // 2, cyc))
 
     def send_half(s, span, sem):
-        own[s, :, span] = acc[mine, span]
         half_send[s, :, span] = acc[other, span].astype(BF16)
         halves.append(
             remote(half_send.at[s, :, span], half_recv.at[s, :, span], half_ss.at[sem], half_rs.at[sem], (r, partner))
         )
+        own[s, :, span] = acc[mine, span]
 
     def send_row(s):
         halves[s].wait()
@@ -223,15 +223,19 @@
                 )
     for copy in later_core:
         copy.wait()
-    halves[rows - 1].wait()
-    halves[rows].wait()
-    summed = own[rows - 1] + half_recv[rows - 1].astype(F32)
+    table = tm[...].reshape(cols * degs, cyc)
+
+    def applied(left, right):
+        return lax.dot_general(left, right, (((1,), (1,)), ((), ())), preferred_element_type=F32)
+
+    summed = own[rows - 1]
     for s in range(rows - 1):
         rowed[s].wait()
         summed = summed + row_recv[s].astype(F32)
-    summed = summed.astype(BF16)
-    table = tm[...].reshape(cols * degs, cyc)
-    product = lax.dot_general(table, summed, (((1,), (1,)), ((), ())), preferred_element_type=F32)
+    product = applied(table, summed.astype(BF16))
+    for h, span in enumerate(spans):
+        halves[rows - 1 + h].wait()
+        product = product + applied(table[:, span], half_recv[rows - 1, :, span])
     op_send[...] = product.astype(BF16).reshape(cols, degs, half)
     sends = []
     for i in range(1, cols):

time: 33.9 us -> 33.3 us (0.982)
  Pallas kernels: 32.4 us -> 31.7 us
    pallas_call x1, Pallas kernels: 32.4 us -> 31.7 us  [per_device(): pl.pallas_call(functools.partial(kernel, rows, cols, chunk), out_shape=ja...]
where the time goes in v4:
time: 33.3 us; the launch traced here: 33.1 us
  Pallas kernels  31.7 us (95%)
  local copies, waits for them, and re-layouts  1.38 us (4%)
    pallas_call x1, Pallas kernels, per_device(): pl.pallas_call(functools.partial(kernel, rows, cols, chunk), out_shape=ja...  31.7 us
    unnamed x1, local copies, waits for them, and re-layouts  1.38 us

profile of v4, /device:TPU:0, one launch (start us, length us, event | category | flops | bytes accessed | tf_op | source)
XLA Modules:
  0.0 33.1 jit_solution(4515785699497439598)
XLA Ops:
  0.0 31.7 %shard_map.55 = bf16[64,256]{1,0:T(8,128)(2,1)} custom-call(bf16[128,64,512]{2,1,0:T(8,128)(2,1)} %t_hbm.1, bf16[128,64,256]{2,1,0:T(8,128)(2,1)} %v_hbm.1, s32[4]{0:T(128)} %order_ref.1, s32[2,512]{1,0:T(2,128)} %bitcast.4, f32[1,512]{1,0:T(1,128)} %bitcast.5), custom_call_target="tpu_custom_call" | custom-call | tf_op jit(solution)/shard_map/pallas_call | solution.py:268
  31.7 1.4 %copy.7 = bf16[64,1,256]{2,0,1:T(8,128)(2,1)} copy(bf16[64,1,256]{2,0,1:T(8,128)(2,1)} %bitcast.3) | data formatting | bytes 65536

commit v5 on v4

--- a/solution.py
+++ b/solution.py
@@ -164,6 +164,7 @@
     halves = []
     rowed = []
 
+    offsets = [q for q in range(1, rows) if q != rows // 2] + [rows // 2, 0]
     spans = (slice(0, cyc // 2), slice(cyc // 2, cyc))
 
     def send_half(s, span, sem):
@@ -176,10 +177,10 @@
     def send_row(s):
         halves[s].wait()
         row_send[s] = (own[s] + half_recv[s].astype(F32)).astype(BF16)
-        rowed.append(remote(row_send.at[s], row_recv.at[s], row_ss.at[s], row_rs.at[s], ((r + s + 1) % rows, c)))
+        rowed.append(remote(row_send.at[s], row_recv.at[s], row_ss.at[s], row_rs.at[s], ((r + offsets[s]) % rows, c)))
 
     for s in range(rows):
-        panel = (r + s + 1) % rows
+        panel = (r + offsets[s]) % rows
         if s == 0:
             first_phase(panel)
             pl.semaphore_wait(barrier, (rows - 1) + (cols - 1))

time: 33.3 us -> 33.4 us (level)
  no operation moved by 1% of the time
where the time goes in v5:
time: 33.4 us; the launch traced here: 33.2 us
  Pallas kernels  31.9 us (96%)
  local copies, waits for them, and re-layouts  1.38 us (4%)
    pallas_call x1, Pallas kernels, per_device(): pl.pallas_call(functools.partial(kernel, rows, cols, chunk), out_shape=ja...  31.9 us
    unnamed x1, local copies, waits for them, and re-layouts  1.38 us

profile of v5, /device:TPU:0, one launch (start us, length us, event | category | flops | bytes accessed | tf_op | source)
XLA Modules:
  0.0 33.2 jit_solution(11684366349744511698)
XLA Ops:
  0.0 31.9 %shard_map.55 = bf16[64,256]{1,0:T(8,128)(2,1)} custom-call(bf16[128,64,512]{2,1,0:T(8,128)(2,1)} %t_hbm.1, bf16[128,64,256]{2,1,0:T(8,128)(2,1)} %v_hbm.1, s32[4]{0:T(128)} %order_ref.1, s32[2,512]{1,0:T(2,128)} %bitcast.4, f32[1,512]{1,0:T(1,128)} %bitcast.5), custom_call_target="tpu_custom_call" | custom-call | tf_op jit(solution)/shard_map/pallas_call | solution.py:269
  31.9 1.4 %copy.7 = bf16[64,1,256]{2,0,1:T(8,128)(2,1)} copy(bf16[64,1,256]{2,0,1:T(8,128)(2,1)} %bitcast.3) | data formatting | bytes 65536
